TPU v7x, 32 devices: a whole 2x2x4 slice. The times are simulated.
32 devices in a mesh: dp: 16 (over z, y, x), mp: 2 (over core).
Axes of the slice: x: 2, y: 2, z: 4, core: 2. Of those that a mesh axis runs over, the one named last changes fastest.
Arguments:
- gradient: bfloat16 [2, 8, 512, 512], P('mp', None, 'dp'), may hold values from -54 to 54
- owners: int32 [2, 8], P('mp'), may hold values from 0 to 15, as said below
- left_stats: float32 [2, 16, 512, 512], P('mp', 'dp'), may hold values from -0.2 to 20.2
- right_stats: float32 [2, 16, 512, 512], P('mp', 'dp'), may hold values from -0.2 to 20.2
- left_roots_old: bfloat16 [2, 16, 512, 512], P('mp', 'dp'), may hold values from -0.1 to 1.5
- right_roots_old: bfloat16 [2, 16, 512, 512], P('mp', 'dp'), may hold values from -0.1 to 1.5
Outputs:
- update: bfloat16 [2, 8, 512, 512], P('mp', None, 'dp')
- left_roots: bfloat16 [2, 16, 512, 512], P('mp', 'dp')
- right_roots: bfloat16 [2, 16, 512, 512], P('mp', 'dp')
Inputs may be any that keep to these rules, and one draw needn't show every extreme that they name: In each row the 8 owners are distinct. Owner o holds a block of row m exactly when owner (o + 8) mod 16 of row m holds none, and exactly when owner o of row (m + 1) mod 2 holds none.
All inputs are finite; a program needn't handle non-finite values.
Results may differ from a plain program's by a relative error of at most 0.0067.
Values may be sent and summed in bfloat16 or wider, within the bound.
A program may use at most 64 MiB of HBM per device.

v0:
```python
import jax
import jax.numpy as jnp
from jax import lax
from jax.sharding import PartitionSpec as P

ITERS = 2
stat_decay = 0.9
ridge_term = 0.001
tiny_term = 1e-06


def newton_root(statistic):
    dimension = statistic.shape[0]
    identity = jnp.eye(dimension, dtype=jnp.float32)
    shifted = statistic + ridge_term * identity
    norm_scale = jnp.sqrt(jnp.sum(shifted * shifted) + tiny_term)
    matrix = shifted / norm_scale
    iterate = identity
    for iteration in range(ITERS):
        factor = ((5.0 * identity - matrix) / 4.0).astype(jnp.bfloat16)
        if iteration == 0:
            iterate = norm_scale ** (-0.25) * lax.optimization_barrier(factor).astype(jnp.float32)
        else:
            iterate = jnp.dot(
                iterate.astype(jnp.bfloat16), factor, preferred_element_type=jnp.float32
            )
        if iteration + 1 < ITERS:
            factor_two = jnp.dot(factor, factor, preferred_element_type=jnp.float32).astype(
                jnp.bfloat16
            )
            factor_four = jnp.dot(
                factor_two, factor_two, preferred_element_type=jnp.float32
            ).astype(jnp.bfloat16)
            matrix = jnp.dot(
                factor_four, matrix.astype(jnp.bfloat16), preferred_element_type=jnp.float32
            )
    return iterate.astype(jnp.bfloat16)


def shards(gradient, owners, left_stats, right_stats, left_roots_old, right_roots_old):
    dp_count = lax.axis_size("dp")
    my_index = lax.axis_index("dp")
    blocks_here = gradient.shape[1]
    row_count = gradient.shape[2]
    block_width = gradient.shape[3]
    owner_table = owners[0]
    owner_ids = jnp.arange(dp_count, dtype=jnp.int32)
    selector = (owner_table[None, :] == owner_ids[:, None]).astype(jnp.bfloat16)
    flat_grad = gradient[0].reshape(blocks_here, row_count * block_width)
    outgoing = jnp.dot(selector, flat_grad, preferred_element_type=jnp.float32).astype(jnp.bfloat16)
    outgoing = outgoing.reshape(dp_count, row_count, block_width)
    arrived = lax.all_to_all(outgoing, "dp", split_axis=0, concat_axis=1, tiled=True)
    grad_block = arrived[0]
    is_mine = owner_table == my_index
    mine_weight = is_mine.astype(jnp.float32)
    is_busy = jnp.any(is_mine)
    left_gram = jnp.einsum("ik,jk->ij", grad_block, grad_block, preferred_element_type=jnp.float32)
    right_gram = jnp.einsum("ki,kj->ij", grad_block, grad_block, preferred_element_type=jnp.float32)
    left_new = stat_decay * left_stats[0, 0] + left_gram / block_width
    right_new = stat_decay * right_stats[0, 0] + right_gram / block_width
    shaded = jnp.dot(grad_block, right_roots_old[0, 0], preferred_element_type=jnp.float32).astype(
        jnp.bfloat16
    )
    direction = jnp.dot(left_roots_old[0, 0], shaded, preferred_element_type=jnp.float32).astype(
        jnp.bfloat16
    )
    squares = jnp.stack(
        [
            jnp.sum(jnp.square(grad_block.astype(jnp.float32))),
            jnp.sum(jnp.square(direction.astype(jnp.float32))),
        ]
    )
    graft_terms = squares[:, None] * mine_weight[None, :]
    returned = lax.all_to_all(direction[None], "dp", split_axis=1, concat_axis=0, tiled=True)
    totals = lax.psum(graft_terms, ("dp", "mp"))
    graft_scale = jnp.sqrt(totals[0] / (totals[1] + tiny_term))
    pieces = jnp.einsum(
        "on,or->nr",
        selector,
        returned.reshape(dp_count, row_count * block_width),
        preferred_element_type=jnp.float32,
    )
    update = (
        (graft_scale[:, None] * pieces)
        .astype(jnp.bfloat16)
        .reshape(1, blocks_here, row_count, block_width)
    )
    zero_root = jnp.zeros((block_width, block_width), jnp.bfloat16)
    left_root, right_root = lax.cond(
        is_busy,
        lambda: (newton_root(left_new), newton_root(right_new)),
        lambda: (zero_root, zero_root),
    )
    return (update, left_root[None, None], right_root[None, None])


def solution(mesh):
    return jax.shard_map(
        shards,
        mesh=mesh,
        in_specs=(
            P("mp", None, "dp", None),
            P("mp", None),
            P("mp", "dp", None, None),
            P("mp", "dp", None, None),
            P("mp", "dp", None, None),
            P("mp", "dp", None, None),
        ),
        out_specs=(P("mp", None, "dp", None), P("mp", "dp", None, None), P("mp", "dp", None, None)),
        check_vma=False,
    )
```

profile of v0, /device:TPU:0, one launch (start us, length us, event | category | flops | bytes accessed | tf_op | source)
XLA Modules:
  0.0 111.4 jit_solution(4444039082128814350)
XLA Ops:
  0.6 0.0 copy-start
  0.6 1.2 %copy.18 = bf16[1,8,32,512]{3,1,2,0:T(8,128)(2,1)S(1)} copy(bf16[1,8,32,512]{3,2,1,0:T(8,128)(2,1)} %param.8) | data formatting | bytes 524288
  1.8 0.0 copy-start.4
  1.8 0.6 copy-done.4
  2.5 0.3 convolution_convert_fusion.6
  2.7 1.0 copy.19
  3.7 0.0 copy-start.5
  3.7 8.5 %all-to-all-start = ((bf16[16,32,512]{2,1,0:T(8,128)(2,1)}), bf16[16,32,512]{2,1,0:T(8,128)(2,1)S(1)}, u32[]{:S(2)}, u32[]{:S(2)}) async-start(bf16[16,32,512]{2,1,0:T(8,128)(2,1)} %bitcast.21), calls=%async_computation | async-start | bytes 1048576 | tf_op jit(solution)/shard_map/all_to_all | solution.py:52
  12.2 0.6 compare_reduce_fusion
  12.8 14.4 %all-to-all-done = bf16[16,32,512]{2,1,0:T(8,128)(2,1)S(1)} async-done(((bf16[16,32,512]{2,1,0:T(8,128)(2,1)}), bf16[16,32,512]{2,1,0:T(8,128)(2,1)S(1)}, u32[]{:S(2)}, u32[]{:S(2)}) %all-to-all-start) | async-done | bytes 524320 | tf_op jit(solution)/shard_map/all_to_all | solution.py:52
  27.3 0.0 copy-done
  27.3 0.0 copy-done.5
  27.3 1.5 %multiply_reduce_fusion.2 = (f32[]{:T(128)}, bf16[512,512]{1,0:T(8,128)(2,1)S(1)}) fusion(bf16[1,1,512,512]{3,2,1,0:T(8,128)(2,1)S(1)} %copy-done, bf16[512,512]{1,0:T(8,128)(2,1)S(1)} %bitcast.76, bf16[1,1,512,512]{3,2,1,0:T(8,128)(2,1)S(1)} %copy-done.5), kind=kOutput, calls=%fused_computation.53 | convolution fusion | flops 538181632 | bytes 2097156 | tf_op jit(solution)/shard_map/dot_general | solution.py:64
  28.8 0.9 copy.16
  29.7 0.5 broadcast.160
  30.2 3.8 %reduce.3 = bf16[512,512]{1,0:T(8,128)(2,1)S(1)} reduce(bf16[512,1,512]{2,1,0:T(2,128)(2,1)S(1)} %bitcast.78, bf16[]{:T(256)} %broadcast.160), dimensions={1}, to_apply=%bitcast.56.reduce_sub_computation | reduce | bytes 1048578
  34.0 1.2 %reshape.49 = bf16[16,2,8192]{2,1,0:T(2,128)(2,1)} reshape(bf16[512,512]{1,0:T(8,128)(2,1)S(1)} %reduce.3) | data formatting | bytes 1048576
  35.2 4.2 %all-to-all-start.1 = ((bf16[16,2,8192]{2,1,0:T(2,128)(2,1)}), bf16[16,2,8192]{2,1,0:T(2,128)(2,1)}, u32[]{:S(2)}, u32[]{:S(2)}) async-start(bf16[16,2,8192]{2,1,0:T(2,128)(2,1)} %reshape.49), calls=%async_computation.1 | async-start | bytes 1048576 | tf_op jit(solution)/shard_map/all_to_all | solution.py:74
  39.5 0.9 multiply_reduce_fusion.3
  40.3 1.4 %pad_maximum_fusion = f32[2]{0:T(128)S(1)} fusion(f32[1]{0:T(128)} %bitcast.6, f32[1]{0:T(128)} %bitcast.1), kind=kLoop, calls=%fused_computation.63 | loop fusion | flops 2 | bytes 16 | tf_op jit(solution)/shard_map/stack | solution.py:67
  41.7 0.1 broadcast_multiply_fusion
  42.4 40.7 %psum.7 = f32[2,8]{1,0:T(2,128)S(1)} all-reduce(f32[2,8]{1,0:T(2,128)S(1)} %broadcast_multiply_fusion), channel_id=1, replica_groups=mesh['dp'=16,'mp'=2] {'dp','mp'}, use_global_device_ids=true, to_apply=%region_2.0 | all-reduce | flops 16 | bytes 128 | tf_op jit(solution)/shard_map/psum | solution.py:75
  83.1 0.5 fusion.37
  83.6 0.0 copy-start.1
  83.6 1.5 %convolution_bitcast_fusion = f32[512,512]{1,0:T(8,128)} fusion(bf16[16,32,512]{2,1,0:T(8,128)(2,1)S(1)} %all-to-all-done), kind=kOutput, calls=%fused_computation.50 | convolution fusion | flops 268435456 | bytes 1572864 | tf_op jit(solution)/shard_map/ki,kj->ij/dot_general | solution.py:58
  85.1 0.0 copy-done.1
  85.1 18.9 %conditional.1 = (bf16[1,1,512,512]{3,2,1,0:T(8,128)(2,1)S(1)}, bf16[1,1,512,512]{3,2,1,0:T(8,128)(2,1)}) conditional(s32[]{:T(128)} %convert_element_type.101, () %tuple.22, (f32[1,1,512,512]{3,2,1,0:T(8,128)S(1)}, f32[512,512]{1,0:T(8,128)S(1)}, f32[1,1,512,512]{3,2,1,0:T(8,128)}, f32[512,512]{1,0:T(8,128)}) %tuple.39), branch_computations={%region_4.0_spmd, %region_5.0_spmd.clone} | conditional | flops 2166620160 | bytes 20971660 | solution.py:89
  85.1 0.9 multiply_reduce_fusion.1
  86.7 2.4 %multiply_reduce_fusion = f32[]{:T(128)} fusion(f32[512,512]{1,0:T(8,128)} %get-tuple-element.58, f32[1,1,512,512]{3,2,1,0:T(8,128)} %get-tuple-element.60), kind=kLoop, calls=%fused_computation.25 | loop fusion | flops 2097151 | bytes 2097156 | tf_op jit(solution)/shard_map/cond/branch_1_fun/reduce_sum | solution.py:16
  89.8 2.9 %fusion.7 = (bf16[512,512]{1,0:T(8,128)(2,1)S(1)}, bf16[512,512]{1,0:T(8,128)(2,1)}) fusion(f32[]{:T(128)S(6)} %sqrt.20, f32[512,512]{1,0:T(8,128)S(1)} %get-tuple-element.57, f32[1,1,512,512]{3,2,1,0:T(8,128)S(1)} %get-tuple-element.59, f32[]{:T(128)S(6)} %sqrt.21, f32[512,512]{1,0:T(8,128)} %get-tuple-element.58, f32[1,1,512,512]{3,2,1,0:T(8,128)} %get-tuple-element.60), kind=kLoop, calls=%fused_computation.19 | loop fusion | flops 4980736 | bytes 5242888 | tf_op jit(solution)/shard_map/cond/branch_1_fun/convert_element_type | solution.py:20
  92.7 0.0 copy-start.3
  92.7 3.6 %convolution_convert_fusion.1 = bf16[512,512]{1,0:T(8,128)(2,1)} fusion(bf16[512,512]{1,0:T(8,128)(2,1)} %get-tuple-element.75), kind=kOutput, calls=%fused_computation.9 | convolution fusion | flops 537395200 | bytes 1048576 | tf_op jit(solution)/shard_map/cond/branch_1_fun/dot_general | solution.py:31
  96.4 3.5 %fusion.5 = bf16[1,1,512,512]{3,2,1,0:T(8,128)(2,1)} fusion(bf16[512,512]{1,0:T(8,128)(2,1)} %convolution_convert_fusion.1, bf16[512,512]{1,0:T(8,128)(2,1)} %get-tuple-element.75, f32[]{:T(128)S(6)} %pow.9, f32[]{:T(128)S(6)} %sqrt.21, f32[1,1,512,512]{3,2,1,0:T(8,128)} %get-tuple-element.60, f32[512,512]{1,0:T(8,128)} %get-tuple-element.58), kind=kOutput, calls=%fused_computation.17 | convolution fusion | flops 541327360 | bytes 3670024 | tf_op jit(solution)/shard_map/cond/branch_1_fun/dot_general | solution.py:24
  99.9 0.0 copy-done.3
  99.9 1.8 %convolution_convert_fusion.4 = bf16[512,512]{1,0:T(8,128)(2,1)} fusion(bf16[512,512]{1,0:T(8,128)(2,1)S(1)} %get-tuple-element.74), kind=kOutput, calls=%fused_computation.12 | convolution fusion | flops 537395200 | bytes 1048576 | tf_op jit(solution)/shard_map/cond/branch_1_fun/dot_general | solution.py:31
  101.8 2.1 %fusion.4 = bf16[1,1,512,512]{3,2,1,0:T(8,128)(2,1)S(1)} fusion(bf16[512,512]{1,0:T(8,128)(2,1)} %convolution_convert_fusion.4, bf16[512,512]{1,0:T(8,128)(2,1)} %copy-done.3, f32[]{:T(128)S(6)} %pow.8, f32[]{:T(128)S(6)} %sqrt.20, f32[1,1,512,512]{3,2,1,0:T(8,128)S(1)} %get-tuple-element.59, f32[512,512]{1,0:T(8,128)S(1)} %get-tuple-element.57), kind=kOutput, calls=%fused_computation.16 | convolution fusion | flops 541327360 | bytes 3670024 | tf_op jit(solution)/shard_map/cond/branch_1_fun/dot_general | solution.py:24
  104.0 0.0 copy-start.2
  104.0 0.8 copy-done.2
  104.8 0.0 all-to-all-done.1
  104.8 2.2 %reshape.50 = bf16[512,1,512]{2,1,0:T(2,128)(2,1)S(1)} reshape(bf16[16,2,8192]{2,1,0:T(2,128)(2,1)} %all-to-all-done.1) | data formatting | bytes 1048576
  107.0 3.1 %bitcast_reduce_fusion = bf16[512,512]{1,0:T(8,128)(2,1)S(1)} fusion(bf16[512,1,512]{2,1,0:T(2,128)(2,1)S(1)} %reshape.50), kind=kLoop, calls=%fused_computation.67 | loop fusion | bytes 1048576 | tf_op jit(solution)/shard_map/all_to_all | solution.py:74
  110.1 0.2 reshape.40
  110.4 0.3 fusion.28
  110.7 0.8 copy.17
  (2 shorter events, 0.0 us)
Async XLA Ops:
  0.6 26.6 %copy-start = (bf16[1,1,512,512]{3,2,1,0:T(8,128)(2,1)S(1)}, bf16[1,1,512,512]{3,2,1,0:T(8,128)(2,1)}, u32[]{:S(2)}) copy-start(bf16[1,1,512,512]{3,2,1,0:T(8,128)(2,1)} %param.12) | copy-start | bytes 1572868
  1.8 0.7 copy-start.4
  3.7 23.6 %copy-start.5 = (bf16[1,1,512,512]{3,2,1,0:T(8,128)(2,1)S(1)}, bf16[1,1,512,512]{3,2,1,0:T(8,128)(2,1)}, u32[]{:S(2)}) copy-start(bf16[1,1,512,512]{3,2,1,0:T(8,128)(2,1)} %param.13) | copy-start | bytes 1572868
  3.7 23.6 %all-to-all-start = ((bf16[16,32,512]{2,1,0:T(8,128)(2,1)}), bf16[16,32,512]{2,1,0:T(8,128)(2,1)S(1)}, u32[]{:S(2)}, u32[]{:S(2)}) async-start(bf16[16,32,512]{2,1,0:T(8,128)(2,1)} %bitcast.21), calls=%async_computation | async-start | bytes 1048576 | tf_op jit(solution)/shard_map/all_to_all | solution.py:52
  35.2 69.6 %all-to-all-start.1 = ((bf16[16,2,8192]{2,1,0:T(2,128)(2,1)}), bf16[16,2,8192]{2,1,0:T(2,128)(2,1)}, u32[]{:S(2)}, u32[]{:S(2)}) async-start(bf16[16,2,8192]{2,1,0:T(2,128)(2,1)} %reshape.49), calls=%async_computation.1 | async-start | bytes 1048576 | tf_op jit(solution)/shard_map/all_to_all | solution.py:74
  83.6 1.5 %copy-start.1 = (f32[1,1,512,512]{3,2,1,0:T(8,128)S(1)}, f32[1,1,512,512]{3,2,1,0:T(8,128)}, u32[]{:S(2)}) copy-start(f32[1,1,512,512]{3,2,1,0:T(8,128)} %param.10) | copy-start | bytes 3145732
  92.7 7.2 %copy-start.3 = (bf16[512,512]{1,0:T(8,128)(2,1)}, bf16[512,512]{1,0:T(8,128)(2,1)S(1)}, u32[]{:S(2)}) copy-start(bf16[512,512]{1,0:T(8,128)(2,1)S(1)} %get-tuple-element.74) | copy-start | bytes 1572868 | tf_op jit(solution)/shard_map/cond
  104.0 0.8 copy-start.2
where the time goes:
time: 112 us; the launch traced here: 111 us
  blocking collectives  40.7 us (36%)
  matrix products  15 us (13%)
  waiting for transfers between devices  14.4 us (13%)
  other arithmetic  13 us (12%)
  starting transfers between devices  12.7 us (11%)
  local copies, waits for them, and re-layouts  12.5 us (11%)
  loops' own time  1.68 us (2%)
  between operations  1.41 us (1%)
    psum x1, blocking collectives, shards(): totals = lax.psum(graft_terms, ('dp', 'mp'))  40.7 us
    all_to_all x1, waiting for transfers between devices, shards(): lax.all_to_all(outgoing, 'dp', split_axis=0, concat_axis=1, tiled=True)  14.4 us
    all_to_all x1, starting transfers between devices, shards(): lax.all_to_all(outgoing, 'dp', split_axis=0, concat_axis=1, tiled=True)  8.47 us
    unnamed x16, local copies, waits for them, and re-layouts  8.25 us
    dot_general x2, matrix products, newton_root(): jnp.dot(iterate.astype(jnp.bfloat16), factor, preferred_element_type=jnp....  5.58 us
    dot_general x2, matrix products, newton_root(): jnp.dot(factor_two, factor_two, preferred_element_type=jnp.float32)  5.42 us
    all_to_all x1, starting transfers between devices, shards(): lax.all_to_all(direction[None], 'dp', split_axis=1, concat_axis=0, tiled=...  4.23 us
    unnamed x1, other arithmetic  3.82 us
  transfers between devices with their start and end apart: 2, of which 1 were waited for; matrix products, arithmetic and copies ran while one was open for 20% of the time, Pallas kernels for 0%

commit v1 on v0

--- a/solution.py
+++ b/solution.py
@@ -49,7 +49,10 @@
     flat_grad = gradient[0].reshape(blocks_here, row_count * block_width)
     outgoing = jnp.dot(selector, flat_grad, preferred_element_type=jnp.float32).astype(jnp.bfloat16)
     outgoing = outgoing.reshape(dp_count, row_count, block_width)
-    arrived = lax.all_to_all(outgoing, "dp", split_axis=0, concat_axis=1, tiled=True)
+    arrived = jnp.concatenate(
+        lax.all_to_all(jnp.stack(jnp.split(outgoing, lax.axis_size("dp"), axis=0)), "dp", 0, 0),
+        axis=1,
+    )
     grad_block = arrived[0]
     is_mine = owner_table == my_index
     mine_weight = is_mine.astype(jnp.float32)

time: 112 us -> 123 us (1.098)
  local copies, waits for them, and re-layouts: 12.5 us -> 23.9 us
    unnamed x16 -> x28, local copies, waits for them, and re-layouts: 8.25 us -> 15.8 us
    split x0 -> x1, local copies, waits for them, and re-layouts: none -> 2.8 us  [shards(): jnp.split(outgoing, lax.axis_size('dp'), axis=0)]
  transfers between devices with their start and end apart: 2 -> 2, of which waited for: 1 -> 1; matrix products, arithmetic and copies ran while one was open for 20% -> 18% of each run, Pallas kernels for 0% -> 0%
where the time goes in v1:
time: 123 us
  blocking collectives  40.7 us (33%)
  local copies, waits for them, and re-layouts  23.9 us (19%)
  matrix products  14.8 us (12%)
  waiting for transfers between devices  14.4 us (12%)
  other arithmetic  13.1 us (11%)
  starting transfers between devices  12.7 us (10%)
  loops' own time  1.53 us (1%)
  between operations  1.52 us (1%)
    psum x1, blocking collectives, shards(): totals = lax.psum(graft_terms, ('dp', 'mp'))  40.7 us
    unnamed x28, local copies, waits for them, and re-layouts  15.8 us
    all_to_all x1, waiting for transfers between devices, shards(): lax.all_to_all(jnp.stack(jnp.split(outgoing, lax.axis_size('dp'), axis=0)...  14.4 us
    all_to_all x1, starting transfers between devices, shards(): lax.all_to_all(jnp.stack(jnp.split(outgoing, lax.axis_size('dp'), axis=0)...  8.47 us
    dot_general x2, matrix products, newton_root(): jnp.dot(factor_two, factor_two, preferred_element_type=jnp.float32)  5.44 us
    dot_general x2, matrix products, newton_root(): jnp.dot(iterate.astype(jnp.bfloat16), factor, preferred_element_type=jnp....  5.39 us
    all_to_all x1, starting transfers between devices, shards(): lax.all_to_all(direction[None], 'dp', split_axis=1, concat_axis=0, tiled=...  4.23 us
    unnamed x1, other arithmetic  3.95 us
  transfers between devices with their start and end apart: 2, of which 1 were waited for; matrix products, arithmetic and copies ran while one was open for 18% of the time, Pallas kernels for 0%

profile of v1, /device:TPU:0, one launch (start us, length us, event | category | flops | bytes accessed | tf_op | source)
XLA Modules:
  0.0 122.8 jit_solution(4613704231016658092)
XLA Ops:
  0.6 0.0 copy-start
  0.6 1.2 copy.50
  1.8 0.0 copy-start.5
  1.8 0.6 copy-done.5
  2.5 0.3 convolution_convert_fusion.6
  2.7 2.8 %slice_reduce_fusion = (bf16[16384]{0:T(1024)(128)(2,1)S(1)}, bf16[16384]{0:T(1024)(128)(2,1)S(1)}, bf16[16384]{0:T(1024)(128)(2,1)S(1)}, bf16[16384]{0:T(1024)(...) fusion(bf16[16,16384]{1,0:T(8,128)(2,1)S(1)} %convolution_conve, ...), kind=kLoop, calls=%fused_computation.58 | loop fusion | bytes 1048576 | tf_op jit(solution)/shard_map/split | solution.py:53
  5.6 0.6 constant_dynamic-update-slice_fusion.15
  6.8 0.6 constant_dynamic-update-slice_fusion.14
  7.4 0.6 constant_dynamic-update-slice_fusion.13
  8.0 0.6 constant_dynamic-update-slice_fusion.12
  8.7 0.6 constant_dynamic-update-slice_fusion.11
  9.3 0.6 constant_dynamic-update-slice_fusion.10
  9.9 0.6 constant_dynamic-update-slice_fusion.9
  10.5 0.6 constant_dynamic-update-slice_fusion.8
  11.1 0.6 constant_dynamic-update-slice_fusion.7
  11.7 0.6 constant_dynamic-update-slice_fusion.6
  12.4 0.6 constant_dynamic-update-slice_fusion.5
  13.0 0.6 constant_dynamic-update-slice_fusion.4
  13.6 0.6 constant_dynamic-update-slice_fusion.3
  14.2 0.6 constant_dynamic-update-slice_fusion.2
  14.8 0.6 constant_dynamic-update-slice_fusion.1
  15.4 0.6 constant_dynamic-update-slice_fusion
  16.1 0.0 copy-start.6
  16.1 8.5 %all-to-all-start = ((bf16[16,1,32,512]{3,2,1,0:T(8,128)(2,1)}), bf16[16,1,32,512]{3,2,1,0:T(8,128)(2,1)S(1)}, u32[]{:S(2)}, u32[]{:S(2)}) async-start(bf16[16,1,32,512]{3,2,1,0:T(8,128)(2,1)} %constant_dynamic-update-slice_fusion), calls=%async_computation | async-start | bytes 1048576 | tf_op jit(solution)/shard_map/all_to_all | solution.py:53
  24.6 0.6 compare_reduce_fusion
  25.2 14.4 %all-to-all-done = bf16[16,1,32,512]{3,2,1,0:T(8,128)(2,1)S(1)} async-done(((bf16[16,1,32,512]{3,2,1,0:T(8,128)(2,1)}), bf16[16,1,32,512]{3,2,1,0:T(8,128)(2,1)S(1)}, u32[]{:S(2)}, u32[]{:S(2)}) %all-to-all-start) | async-done | bytes 524320 | tf_op jit(solution)/shard_map/all_to_all | solution.py:53
  39.6 0.0 copy-done
  39.6 0.0 copy-done.6
  39.6 1.5 %multiply_reduce_fusion.2 = (f32[]{:T(128)}, bf16[512,512]{1,0:T(8,128)(2,1)S(1)}) fusion(bf16[1,1,512,512]{3,2,1,0:T(8,128)(2,1)S(1)} %copy-done, bf16[512,512]{1,0:T(8,128)(2,1)S(1)} %bitcast.75, bf16[1,1,512,512]{3,2,1,0:T(8,128)(2,1)S(1)} %copy-done.6), kind=kOutput, calls=%fused_computation.53 | convolution fusion | flops 538181632 | bytes 2097156 | tf_op jit(solution)/shard_map/dot_general | solution.py:67
  41.2 0.9 copy.48
  42.1 0.5 broadcast.176
  42.6 4.0 %reduce.35 = bf16[512,512]{1,0:T(8,128)(2,1)S(1)} reduce(bf16[512,1,512]{2,1,0:T(2,128)(2,1)S(1)} %bitcast.77, bf16[]{:T(256)} %broadcast.176), dimensions={1}, to_apply=%bitcast.57.reduce_sub_computation | reduce | bytes 1048578
  46.5 1.2 reshape.95
  47.7 4.2 %all-to-all-start.1 = ((bf16[16,2,8192]{2,1,0:T(2,128)(2,1)}), bf16[16,2,8192]{2,1,0:T(2,128)(2,1)}, u32[]{:S(2)}, u32[]{:S(2)}) async-start(bf16[16,2,8192]{2,1,0:T(2,128)(2,1)} %reshape.95), calls=%async_computation.1 | async-start | bytes 1048576 | tf_op jit(solution)/shard_map/all_to_all | solution.py:77
  52.0 0.9 multiply_reduce_fusion.3
  52.8 1.4 %pad_maximum_fusion = f32[2]{0:T(128)S(1)} fusion(f32[1]{0:T(128)} %bitcast.6, f32[1]{0:T(128)} %bitcast.1), kind=kLoop, calls=%fused_computation.96 | loop fusion | flops 2 | bytes 16 | tf_op jit(solution)/shard_map/stack | solution.py:70
  54.2 0.1 broadcast_multiply_fusion
  54.9 40.7 %psum.7 = f32[2,8]{1,0:T(2,128)S(1)} all-reduce(f32[2,8]{1,0:T(2,128)S(1)} %broadcast_multiply_fusion), channel_id=1, replica_groups=mesh['dp'=16,'mp'=2] {'dp','mp'}, use_global_device_ids=true, to_apply=%region_2.0 | all-reduce | flops 16 | bytes 128 | tf_op jit(solution)/shard_map/psum | solution.py:78
  95.6 0.5 fusion.38
  96.1 0.0 copy-start.1
  96.1 1.5 %convolution_bitcast_fusion = f32[512,512]{1,0:T(8,128)} fusion(bf16[16,1,32,512]{3,2,1,0:T(8,128)(2,1)S(1)} %all-to-all-done), kind=kOutput, calls=%fused_computation.50 | convolution fusion | flops 268435456 | bytes 1572864 | tf_op jit(solution)/shard_map/ki,kj->ij/dot_general | solution.py:61
  97.6 0.0 copy-done.1
  97.6 18.6 %conditional.1 = (bf16[1,1,512,512]{3,2,1,0:T(8,128)(2,1)}, bf16[1,1,512,512]{3,2,1,0:T(8,128)(2,1)}) conditional(s32[]{:T(128)} %convert_element_type.101, () %tuple.22, (f32[1,1,512,512]{3,2,1,0:T(8,128)S(1)}, f32[512,512]{1,0:T(8,128)S(1)}, f32[1,1,512,512]{3,2,1,0:T(8,128)}, f32[512,512]{1,0:T(8,128)}) %tuple.54), branch_computations={%region_4.0_spmd, %region_5.0_spmd.clone} | conditional | flops 2166620160 | bytes 29360324 | solution.py:92
  97.6 0.9 multiply_reduce_fusion.1
  99.2 2.4 %multiply_reduce_fusion = f32[]{:T(128)} fusion(f32[512,512]{1,0:T(8,128)} %get-tuple-element.58, f32[1,1,512,512]{3,2,1,0:T(8,128)} %get-tuple-element.60), kind=kLoop, calls=%fused_computation.25 | loop fusion | flops 2097151 | bytes 2097156 | tf_op jit(solution)/shard_map/cond/branch_1_fun/reduce_sum | solution.py:16
  102.3 2.9 %fusion.7 = (bf16[512,512]{1,0:T(8,128)(2,1)S(1)}, bf16[512,512]{1,0:T(8,128)(2,1)}) fusion(f32[]{:T(128)S(6)} %sqrt.20, f32[512,512]{1,0:T(8,128)S(1)} %get-tuple-element.57, f32[1,1,512,512]{3,2,1,0:T(8,128)S(1)} %get-tuple-element.59, f32[]{:T(128)S(6)} %sqrt.21, f32[512,512]{1,0:T(8,128)} %get-tuple-element.58, f32[1,1,512,512]{3,2,1,0:T(8,128)} %get-tuple-element.60), kind=kLoop, calls=%fused_computation.19 | loop fusion | flops 4980736 | bytes 5242888 | tf_op jit(solution)/shard_map/cond/branch_1_fun/convert_element_type | solution.py:20
  105.1 1.9 %convolution_convert_fusion.4 = bf16[512,512]{1,0:T(8,128)(2,1)} fusion(bf16[512,512]{1,0:T(8,128)(2,1)S(1)} %get-tuple-element.90), kind=kOutput, calls=%fused_computation.12 | convolution fusion | flops 537395200 | bytes 1048576 | tf_op jit(solution)/shard_map/cond/branch_1_fun/dot_general | solution.py:31
  107.1 2.7 %fusion.4 = bf16[1,1,512,512]{3,2,1,0:T(8,128)(2,1)} fusion(bf16[512,512]{1,0:T(8,128)(2,1)} %convolution_convert_fusion.4, bf16[512,512]{1,0:T(8,128)(2,1)S(1)} %get-tuple-element.90, f32[]{:T(128)S(6)} %pow.8, f32[]{:T(128)S(6)} %sqrt.20, f32[1,1,512,512]{3,2,1,0:T(8,128)S(1)} %get-tuple-element.59, f32[512,512]{1,0:T(8,128)S(1)} %get-tuple-element.57), kind=kOutput, calls=%fused_computation.16 | convolution fusion | flops 541327360 | bytes 3670024 | tf_op jit(solution)/shard_map/cond/branch_1_fun/dot_general | solution.py:24
  109.8 0.0 copy-start.2
  109.8 0.0 copy-start.3
  109.8 0.0 copy-start.4
  109.8 3.6 %convolution_convert_fusion.1 = bf16[512,512]{1,0:T(8,128)(2,1)} fusion(bf16[512,512]{1,0:T(8,128)(2,1)} %get-tuple-element.91), kind=kOutput, calls=%fused_computation.9 | convolution fusion | flops 537395200 | bytes 1048576 | tf_op jit(solution)/shard_map/cond/branch_1_fun/dot_general | solution.py:31
  113.4 0.0 copy-done.2
  113.4 0.0 copy-done.3
  113.4 0.0 copy-done.4
  113.4 2.7 %fusion.5 = bf16[1,1,512,512]{3,2,1,0:T(8,128)(2,1)} fusion(bf16[512,512]{1,0:T(8,128)(2,1)} %convolution_convert_fusion.1, bf16[512,512]{1,0:T(8,128)(2,1)S(1)} %copy-done.4, f32[]{:T(128)S(6)} %pow.9, f32[]{:T(128)S(6)} %sqrt.21, f32[1,1,512,512]{3,2,1,0:T(8,128)S(1)} %copy-done.2, f32[512,512]{1,0:T(8,128)S(1)} %copy-done.3), kind=kOutput, calls=%fused_computation.17 | convolution fusion | flops 541327360 | bytes 3670024 | tf_op jit(solution)/shard_map/cond/branch_1_fun/dot_general | solution.py:24
  116.1 0.0 all-to-all-done.1
  116.1 2.2 %reshape.96 = bf16[512,1,512]{2,1,0:T(2,128)(2,1)S(1)} reshape(bf16[16,2,8192]{2,1,0:T(2,128)(2,1)} %all-to-all-done.1) | data formatting | bytes 1048576
  118.4 3.1 %bitcast_reduce_fusion = bf16[512,512]{1,0:T(8,128)(2,1)S(1)} fusion(bf16[512,1,512]{2,1,0:T(2,128)(2,1)S(1)} %reshape.96), kind=kLoop, calls=%fused_computation.100 | loop fusion | bytes 1048576 | tf_op jit(solution)/shard_map/all_to_all | solution.py:77
  121.5 0.2 reshape.69
  121.7 0.3 fusion.28
  122.0 0.8 copy.49
  (18 shorter events, 0.5 us)
Async XLA Ops:
  0.6 39.0 %copy-start = (bf16[1,1,512,512]{3,2,1,0:T(8,128)(2,1)S(1)}, bf16[1,1,512,512]{3,2,1,0:T(8,128)(2,1)}, u32[]{:S(2)}) copy-start(bf16[1,1,512,512]{3,2,1,0:T(8,128)(2,1)} %param.12) | copy-start | bytes 1572868
  1.8 0.7 copy-start.5
  16.1 23.6 %copy-start.6 = (bf16[1,1,512,512]{3,2,1,0:T(8,128)(2,1)S(1)}, bf16[1,1,512,512]{3,2,1,0:T(8,128)(2,1)}, u32[]{:S(2)}) copy-start(bf16[1,1,512,512]{3,2,1,0:T(8,128)(2,1)} %param.13) | copy-start | bytes 1572868
  16.1 23.6 %all-to-all-start = ((bf16[16,1,32,512]{3,2,1,0:T(8,128)(2,1)}), bf16[16,1,32,512]{3,2,1,0:T(8,128)(2,1)S(1)}, u32[]{:S(2)}, u32[]{:S(2)}) async-start(bf16[16,1,32,512]{3,2,1,0:T(8,128)(2,1)} %constant_dynamic-update-slice_fusion), calls=%async_computation | async-start | bytes 1048576 | tf_op jit(solution)/shard_map/all_to_all | solution.py:53
  47.7 68.4 %all-to-all-start.1 = ((bf16[16,2,8192]{2,1,0:T(2,128)(2,1)}), bf16[16,2,8192]{2,1,0:T(2,128)(2,1)}, u32[]{:S(2)}, u32[]{:S(2)}) async-start(bf16[16,2,8192]{2,1,0:T(2,128)(2,1)} %reshape.95), calls=%async_computation.1 | async-start | bytes 1048576 | tf_op jit(solution)/shard_map/all_to_all | solution.py:77
  96.1 1.5 %copy-start.1 = (f32[1,1,512,512]{3,2,1,0:T(8,128)S(1)}, f32[1,1,512,512]{3,2,1,0:T(8,128)}, u32[]{:S(2)}) copy-start(f32[1,1,512,512]{3,2,1,0:T(8,128)} %param.10) | copy-start | bytes 3145732
  109.8 3.6 %copy-start.2 = (f32[1,1,512,512]{3,2,1,0:T(8,128)S(1)}, f32[1,1,512,512]{3,2,1,0:T(8,128)}, u32[]{:S(2)}) copy-start(f32[1,1,512,512]{3,2,1,0:T(8,128)} %get-tuple-element.60) | copy-start | bytes 3145732 | tf_op jit(solution)/shard_map/cond
  109.8 3.7 %copy-start.3 = (f32[512,512]{1,0:T(8,128)S(1)}, f32[512,512]{1,0:T(8,128)}, u32[]{:S(2)}) copy-start(f32[512,512]{1,0:T(8,128)} %get-tuple-element.58) | copy-start | bytes 3145732 | tf_op jit(solution)/shard_map/cond
  109.8 3.7 %copy-start.4 = (bf16[512,512]{1,0:T(8,128)(2,1)S(1)}, bf16[512,512]{1,0:T(8,128)(2,1)}, u32[]{:S(2)}) copy-start(bf16[512,512]{1,0:T(8,128)(2,1)} %get-tuple-element.91) | copy-start | bytes 1572868 | tf_op jit(solution)/shard_map/cond
